TPU v7x, 32 devices: a whole 2x2x4 slice. The times are simulated.
32 devices in a mesh: groups: 2 (over x), tensor: 16 (over z, y, core).
Axes of the slice: x: 2, y: 2, z: 4, core: 2. Of those that a mesh axis runs over, the one named last changes fastest.
Arguments:
- tokens: bfloat16 [1024, 8192], P('groups', 'tensor'), parts along dimension 0, may hold values from -6 to 6
- norm_gain: float32 [8192], P('tensor'), may hold values from 0.1 to 1.9
- w_in: bfloat16 [8192, 3, 8192], P(None, None, 'tensor'), may hold values from -0.0625 to 0.0625
- w_short: float32 [3, 3, 8192], P(None, None, 'tensor'), may hold values from -3 to 3
- filters: bfloat16 [512, 128], P('tensor'), may hold values from -0.5 to 0.5
- skip: float32 [8192], P('tensor'), may hold values from -4 to 4
- w_out: bfloat16 [8192, 8192], P('tensor'), may hold values from -0.0625 to 0.0625
Outputs:
- mixed: bfloat16 [1024, 8192], P('groups', 'tensor'), parts along dimension 0
There are 2 independent parts, one for each index of `groups`. A program takes and returns all parts, laid end to end along the dimension named above; an argument that names none is the same for every part. Nothing has to cross between parts.
All inputs are finite; a program needn't handle non-finite values.
Results may differ from a plain program's by a relative error of at most 0.0085.
Values may be sent and summed in bfloat16 or wider, within the bound.
A program may use at most 192 MiB of HBM per device.

v0:
```python
import jax
import jax.numpy as jnp
from jax import lax
from jax.sharding import PartitionSpec as P

D = 8192


def shifted(field, lag):
    pads = ((lag, 0),) + ((0, 0),) * (field.ndim - 1)
    return jnp.pad(field, pads)[: field.shape[0]]


def lag_matrix(filters, rows):
    count, taps = filters.shape
    length = taps + rows
    line = jnp.concatenate([filters, jnp.zeros((count, rows), filters.dtype)], axis=1)
    tiled = jnp.tile(line, (1, rows))[:, : rows * (length - 1)]
    return tiled.reshape(count, rows, length - 1)[:, :, :rows]


def on_device(tokens, norm_gain, w_in, w_short, filters, skip, w_out):
    wide = tokens.astype(jnp.float32)
    squares = lax.psum(jnp.sum(wide * wide, axis=1, keepdims=True), "tensor")
    factor = lax.rsqrt(squares / D + 1e-05)
    normed = (wide * factor * norm_gain[None, :]).astype(jnp.bfloat16)
    width = w_in.shape[0]
    local = w_in.shape[2]
    rows = tokens.shape[0]
    w_flat = w_in.reshape(width, 3 * local)
    chosen = w_flat
    proj = jnp.dot(
        lax.all_gather(normed, "tensor", axis=1, tiled=True),
        chosen,
        preferred_element_type=jnp.float32,
    )
    proj = proj.reshape(rows, 3, local)
    short = w_short[0][None] * proj
    for lag in range(1, w_short.shape[0]):
        short = short + w_short[lag][None] * shifted(proj, lag)
    gated = (short[:, 1] * short[:, 2]).astype(jnp.bfloat16)
    count = filters.shape[0]
    lagged = lag_matrix(filters, rows)
    grouped = gated.reshape(rows, count, local // count)
    conv = jnp.einsum("fst,sfg->tfg", lagged, grouped, preferred_element_type=jnp.float32)
    conv = conv.reshape(rows, local)
    hidden = ((conv + skip[None, :] * gated.astype(jnp.float32)) * short[:, 0]).astype(jnp.bfloat16)
    w_cols = lax.all_to_all(w_out, "tensor", split_axis=1, concat_axis=0, tiled=True)
    chosen = w_cols
    summed = jnp.dot(
        lax.all_gather(hidden, "tensor", axis=1, tiled=True),
        chosen,
        preferred_element_type=jnp.float32,
    )
    return (wide + summed).astype(jnp.bfloat16)


def solution(mesh):
    return jax.shard_map(
        on_device,
        mesh=mesh,
        in_specs=(
            P("groups", "tensor"),
            P("tensor"),
            P(None, None, "tensor"),
            P(None, None, "tensor"),
            P("tensor", None),
            P("tensor"),
            P("tensor", None),
        ),
        out_specs=P("groups", "tensor"),
        check_vma=False,
    )
```

profile of v0, /device:TPU:0, one launch (start us, length us, event | category | flops | bytes accessed | tf_op | source)
XLA Modules:
  0.0 382.3 jit_solution(3870038537014596827)
XLA Ops:
  6.5 0.0 all-gather.3.cloned.1.call-start
  6.5 1.2 fusion.10
  7.8 35.0 %psum.7 = f32[512,1]{0,1:T(1,128)S(1)} all-reduce(f32[512,1]{0,1:T(1,128)S(1)} %bitcast.46), channel_id=1, replica_groups=mesh['groups'=2,'tensor'=16] {'tensor'}, use_global_device_ids=true, to_apply=%region_1.0 | all-reduce | flops 512 | bytes 4096 | tf_op jit(solution)/shard_map/psum | solution.py:24
  42.7 2.0 fusion.12
  44.7 0.0 all-gather.3.cloned.1.call-update
  44.8 12.1 %copy.16 = bf16[512,8192]{0,1:T(8,128)(2,1)} copy(bf16[512,8192]{1,0:T(8,128)(2,1)} %param.13) | data formatting | bytes 16777216 | tf_op args[6]
  56.8 4.8 %all-to-all-start = ((bf16[512,16,512]{0,2,1:T(8,128)(2,1)}), bf16[512,16,512]{0,2,1:T(8,128)(2,1)}, u32[]{:S(2)}, u32[]{:S(2)}) async-start(bf16[512,16,512]{0,2,1:T(8,128)(2,1)} %bitcast.41), calls=%async_computation | async-start | bytes 16777216 | tf_op jit(solution)/shard_map/all_to_all | solution.py:48
  61.6 0.0 copy-start.2
  61.6 0.0 all-gather.5.cloned.1.call-start
  61.7 33.5 %copy.13 = bf16[8192,3,512]{0,2,1:T(8,128)(2,1)} copy(bf16[8192,3,512]{2,0,1:T(8,128)(2,1)} %param.9) | data formatting | bytes 50331648 | tf_op args[2]
  95.1 0.0 copy-done.2
  95.1 2.9 tile.4
  98.0 67.1 %copy.18 = bf16[4,8,512,640]{3,1,2,0:T(8,128)(2,1)S(1)} copy(bf16[4,8,512,640]{3,2,1,0:T(8,128)(2,1)S(1)} %bitcast.39) | data formatting | bytes 41943040
  165.1 8.1 %slice.42 = bf16[32,327168]{1,0:T(8,128)(2,1)} slice(bf16[32,327680]{1,0:T(8,128)(2,1)S(1)} %bitcast.40), slice={[0:32], [0:327168]} | slice | bytes 41877504 | tf_op jit(solution)/shard_map/slice | solution.py:18
  173.2 0.0 copy-start.1
  173.2 69.0 %reshape.30 = bf16[32,512,639]{2,1,0:T(8,128)(2,1)} reshape(bf16[32,327168]{1,0:T(8,128)(2,1)} %slice.42) | data formatting | bytes 41877504 | tf_op jit(solution)/shard_map/reshape | solution.py:19
  242.2 0.0 copy-done.1
  242.3 0.0 all-gather.3.cloned.1.call-done
  242.3 19.6 %fusion = f32[512,3,512]{2,0,1:T(8,128)S(1)} fusion(bf16[8192,3,512]{0,2,1:T(8,128)(2,1)} %copy.13, bf16[512,8192]{1,0:T(8,128)(2,1)} %all-gather.3.cloned.1.call-done), kind=kOutput, calls=%fused_computation | convolution fusion | flops 12884901888 | bytes 36700160 | tf_op jit(solution)/shard_map/dot_general | solution.py:32
  261.9 0.9 fusion.7
  262.8 0.9 fusion.15
  263.8 2.1 copy.14
  265.9 0.0 copy-start.3
  265.9 9.2 %fusion.2 = f32[32,16,512]{2,1,0:T(8,128)} fusion(bf16[512,32,16]{0,2,1:T(8,128)(2,1)} %bitcast.44, bf16[32,512,639]{2,1,0:T(8,128)(2,1)} %reshape.30), kind=kOutput, calls=%fused_computation.2 | convolution fusion | flops 268435456 | bytes 18350080 | tf_op jit(solution)/shard_map/fst,sfg->tfg/dot_general | solution.py:45
  275.1 2.6 copy.15
  277.6 0.0 copy-done.3
  277.7 2.5 fusion.14
  280.2 0.0 all-gather.5.cloned.1.call-update
  280.2 0.0 all-to-all-done
  280.2 0.0 copy-start
  280.2 12.4 %copy.17 = bf16[16,512,512]{2,1,0:T(8,128)(2,1)} copy(bf16[16,512,512]{1,2,0:T(8,128)(2,1)} %bitcast.15) | data formatting | bytes 16777216 | tf_op jit(solution)/shard_map/all_to_all | solution.py:48
  292.6 71.8 %all-gather.5.cloned.1.call-done = bf16[512,8192]{1,0:T(8,128)(2,1)} async-done(((bf16[512,512]{1,0:T(8,128)(2,1)}), bf16[512,8192]{1,0:T(8,128)(2,1)}) %all-gather.5.cloned.1.call-update) | async-done | bytes 8388624 | tf_op jit(solution)/shard_map/all_gather | solution.py:51
  364.4 0.0 copy-done
  364.4 11.0 %fusion.9 = bf16[512,512]{1,0:T(8,128)(2,1)} fusion(bf16[512,8192]{1,0:T(8,128)(2,1)} %all-gather.5.cloned.1.call-done, bf16[8192,512]{1,0:T(8,128)(2,1)} %bitcast.43, bf16[512,512]{1,0:T(8,128)(2,1)S(1)} %copy-done), kind=kOutput, calls=%fused_computation.14 | convolution fusion | flops 4295753728 | bytes 17825792 | tf_op jit(solution)/shard_map/dot_general | solution.py:50
  (3 shorter events, 0.0 us)
Async XLA Ops:
  6.5 235.7 %all-gather.3.cloned.1.call-start = ((), (), s32[]{:S(2)}) async-start(), calls=%async_computation.1 | async-start | bytes 8912896 | tf_op jit(solution)/shard_map/all_gather | solution.py:33
  56.8 223.4 %all-to-all-start = ((bf16[512,16,512]{0,2,1:T(8,128)(2,1)}), bf16[512,16,512]{0,2,1:T(8,128)(2,1)}, u32[]{:S(2)}, u32[]{:S(2)}) async-start(bf16[512,16,512]{0,2,1:T(8,128)(2,1)} %bitcast.41), calls=%async_computation | async-start | bytes 16777216 | tf_op jit(solution)/shard_map/all_to_all | solution.py:48
  61.6 33.5 %copy-start.2 = (bf16[32,128]{1,0:T(8,128)(2,1)S(1)}, bf16[32,128]{1,0:T(8,128)(2,1)}, u32[]{:S(2)}) copy-start(bf16[32,128]{1,0:T(8,128)(2,1)} %param.11) | copy-start | bytes 24580
  61.6 302.8 %all-gather.5.cloned.1.call-start = ((), (), s32[]{:S(2)}) async-start(), calls=%async_computation.2 | async-start | bytes 8912896 | tf_op jit(solution)/shard_map/all_gather | solution.py:51
  173.2 69.0 %copy-start.1 = (f32[3,3,512]{2,1,0:T(4,128)S(1)}, f32[3,3,512]{2,1,0:T(4,128)}, u32[]{:S(2)}) copy-start(f32[3,3,512]{2,1,0:T(4,128)} %param.10) | copy-start | bytes 55300
  265.9 11.8 %copy-start.3 = (f32[512]{0:T(512)S(1)}, f32[512]{0:T(512)}, u32[]{:S(2)}) copy-start(f32[512]{0:T(512)} %param.12) | copy-start | bytes 6148
  280.2 84.2 %copy-start = (bf16[512,512]{1,0:T(8,128)(2,1)S(1)}, bf16[512,512]{1,0:T(8,128)(2,1)}, u32[]{:S(2)}) copy-start(bf16[512,512]{1,0:T(8,128)(2,1)} %param.7) | copy-start | bytes 1572868
Sparse Core Ops, SparseCore 0:
  44.9 189.7 all-gather.2
  280.3 84.0 all-gather.4
where the time goes:
time: 384 us; the launch traced here: 382 us
  local copies, waits for them, and re-layouts  210 us (55%)
  waiting for transfers between devices  71.8 us (19%)
  matrix products  39.9 us (10%)
  blocking collectives  35 us (9%)
  between operations  13.5 us (4%)
  other arithmetic  7.65 us (2%)
  starting transfers between devices  4.8 us (1%)
    unnamed x11, local copies, waits for them, and re-layouts  113 us
    all_gather x1, waiting for transfers between devices, on_device(): lax.all_gather(hidden, 'tensor', axis=1, tiled=True)  71.8 us
    reshape x1, local copies, waits for them, and re-layouts, lag_matrix(): return tiled.reshape(count, rows, length - 1)[:, :, :rows]  69 us
    psum x1, blocking collectives, on_device(): squares = lax.psum(jnp.sum(wide * wide, axis=1, keepdims=True), 'tensor')  35 us
    dot_general x1, matrix products, on_device(): jnp.dot(lax.all_gather(normed, 'tensor', axis=1, tiled=True), chosen, pre...  19.6 us
    all_to_all x1, local copies, waits for them, and re-layouts, on_device(): lax.all_to_all(w_out, 'tensor', split_axis=1, concat_axis=0, tiled=True)  12.4 us
    dot_general x1, matrix products, on_device(): jnp.dot(lax.all_gather(hidden, 'tensor', axis=1, tiled=True), chosen, pre...  11 us
    dot_general x1, matrix products, on_device(): jnp.einsum('fst,sfg->tfg', lagged, grouped, preferred_element_type=jnp.fl...  9.22 us
  transfers between devices with their start and end apart: 3, of which 1 were waited for; matrix products, arithmetic and copies ran while one was open for 64% of the time, Pallas kernels for 0%

commit v1 on v0

--- a/solution.py
+++ b/solution.py
@@ -45,7 +45,12 @@
     conv = jnp.einsum("fst,sfg->tfg", lagged, grouped, preferred_element_type=jnp.float32)
     conv = conv.reshape(rows, local)
     hidden = ((conv + skip[None, :] * gated.astype(jnp.float32)) * short[:, 0]).astype(jnp.bfloat16)
-    w_cols = lax.all_to_all(w_out, "tensor", split_axis=1, concat_axis=0, tiled=True)
+    w_cols = jnp.concatenate(
+        lax.all_to_all(
+            jnp.stack(jnp.split(w_out, lax.axis_size("tensor"), axis=1)), "tensor", 0, 0
+        ),
+        axis=0,
+    )
     chosen = w_cols
     summed = jnp.dot(
         lax.all_gather(hidden, "tensor", axis=1, tiled=True),

time: 384 us -> 398 us (1.036)
  waiting for transfers between devices: 71.8 us -> 79 us
  local copies, waits for them, and re-layouts: 210 us -> 215 us
    unnamed x11 -> x23, local copies, waits for them, and re-layouts: 113 us -> 129 us
    all_to_all x1 -> x0, local copies, waits for them, and re-layouts: 12.4 us -> none  [on_device(): lax.all_to_all(w_out, 'tensor', split_axis=1, concat_axis=0, tiled=True)]
    all_gather x1, waiting for transfers between devices: 71.8 us -> 78.9 us  [on_device(): lax.all_gather(hidden, 'tensor', axis=1, tiled=True)]
  transfers between devices with their start and end apart: 3 -> 3, of which waited for: 1 -> 1; matrix products, arithmetic and copies ran while one was open for 64% -> 63% of each run, Pallas kernels for 0% -> 0%
where the time goes in v1:
time: 398 us; the launch traced here: 395 us
  local copies, waits for them, and re-layouts  215 us (54%)
  waiting for transfers between devices  79 us (20%)
  matrix products  39.9 us (10%)
  blocking collectives  35 us (9%)
  between operations  13.5 us (3%)
  other arithmetic  7.65 us (2%)
  starting transfers between devices  4.96 us (1%)
    unnamed x23, local copies, waits for them, and re-layouts  129 us
    all_gather x1, waiting for transfers between devices, on_device(): lax.all_gather(hidden, 'tensor', axis=1, tiled=True)  78.9 us
    reshape x1, local copies, waits for them, and re-layouts, lag_matrix(): return tiled.reshape(count, rows, length - 1)[:, :, :rows]  69 us
    psum x1, blocking collectives, on_device(): squares = lax.psum(jnp.sum(wide * wide, axis=1, keepdims=True), 'tensor')  35 us
    dot_general x1, matrix products, on_device(): jnp.dot(lax.all_gather(normed, 'tensor', axis=1, tiled=True), chosen, pre...  19.6 us
    dot_general x1, matrix products, on_device(): jnp.dot(lax.all_gather(hidden, 'tensor', axis=1, tiled=True), chosen, pre...  11.1 us
    dot_general x1, matrix products, on_device(): jnp.einsum('fst,sfg->tfg', lagged, grouped, preferred_element_type=jnp.fl...  9.23 us
    slice x1, local copies, waits for them, and re-layouts, lag_matrix(): tiled = jnp.tile(line, (1, rows))[:, :rows * (length - 1)]  8.08 us
  transfers between devices with their start and end apart: 3, of which 1 were waited for; matrix products, arithmetic and copies ran while one was open for 63% of the time, Pallas kernels for 0%

profile of v1, /device:TPU:0, one launch (start us, length us, event | category | flops | bytes accessed | tf_op | source)
XLA Modules:
  0.0 395.4 jit_solution(1132656147243223446)
XLA Ops:
  6.5 0.0 all-gather.3.cloned.1.call-start
  6.5 1.2 fusion.10
  7.8 35.0 %psum.7 = f32[512,1]{0,1:T(1,128)S(1)} all-reduce(f32[512,1]{0,1:T(1,128)S(1)} %bitcast.74), channel_id=1, replica_groups=mesh['groups'=2,'tensor'=16] {'tensor'}, use_global_device_ids=true, to_apply=%region_1.0 | all-reduce | flops 512 | bytes 4096 | tf_op jit(solution)/shard_map/psum | solution.py:24
  42.7 2.0 fusion.12
  44.7 0.0 all-gather.3.cloned.1.call-update
  44.8 1.9 bitcast_dynamic-update-slice_fusion.15
  46.7 1.9 bitcast_dynamic-update-slice_fusion.14
  48.5 1.9 bitcast_dynamic-update-slice_fusion.13
  50.5 1.9 bitcast_dynamic-update-slice_fusion.12
  52.4 1.9 bitcast_dynamic-update-slice_fusion.11
  54.3 1.9 bitcast_dynamic-update-slice_fusion.10
  56.1 1.9 bitcast_dynamic-update-slice_fusion.9
  58.0 1.9 bitcast_dynamic-update-slice_fusion.8
  59.9 1.9 bitcast_dynamic-update-slice_fusion.7
  61.7 1.9 bitcast_dynamic-update-slice_fusion.6
  63.6 1.9 bitcast_dynamic-update-slice_fusion.5
  65.5 1.9 bitcast_dynamic-update-slice_fusion.4
  67.4 1.9 bitcast_dynamic-update-slice_fusion.3
  69.2 1.9 bitcast_dynamic-update-slice_fusion.2
  71.1 1.9 bitcast_dynamic-update-slice_fusion.1
  73.0 1.9 bitcast_dynamic-update-slice_fusion
  74.9 4.9 %all-to-all-start = ((bf16[16,512,512]{2,1,0:T(8,128)(2,1)}), bf16[16,512,512]{2,1,0:T(8,128)(2,1)}, u32[]{:S(2)}, u32[]{:S(2)}) async-start(bf16[16,512,512]{2,1,0:T(8,128)(2,1)} %bitcast_dynamic-update-slice_fusion), calls=%async_computation | async-start | bytes 16777216 | tf_op jit(solution)/shard_map/all_to_all | solution.py:49
  79.8 0.0 copy-start.1
  79.8 0.0 all-gather.5.cloned.1.call-start
  79.9 33.6 %copy.10 = bf16[8192,3,512]{0,2,1:T(8,128)(2,1)} copy(bf16[8192,3,512]{2,0,1:T(8,128)(2,1)} %param.9) | data formatting | bytes 50331648 | tf_op args[2]
  113.5 0.0 copy-done.1
  113.5 2.9 tile.4
  116.4 67.1 %copy.13 = bf16[4,8,512,640]{3,1,2,0:T(8,128)(2,1)S(1)} copy(bf16[4,8,512,640]{3,2,1,0:T(8,128)(2,1)S(1)} %bitcast.69) | data formatting | bytes 41943040
  183.5 8.1 %slice.42 = bf16[32,327168]{1,0:T(8,128)(2,1)} slice(bf16[32,327680]{1,0:T(8,128)(2,1)S(1)} %bitcast.70), slice={[0:32], [0:327168]} | slice | bytes 41877504 | tf_op jit(solution)/shard_map/slice | solution.py:18
  191.6 0.0 copy-start
  191.6 69.0 %reshape.30 = bf16[32,512,639]{2,1,0:T(8,128)(2,1)} reshape(bf16[32,327168]{1,0:T(8,128)(2,1)} %slice.42) | data formatting | bytes 41877504 | tf_op jit(solution)/shard_map/reshape | solution.py:19
  260.6 0.0 copy-done
  260.6 0.0 all-gather.3.cloned.1.call-done
  260.6 19.6 %fusion = f32[512,3,512]{2,0,1:T(8,128)S(1)} fusion(bf16[8192,3,512]{0,2,1:T(8,128)(2,1)} %copy.10, bf16[512,8192]{1,0:T(8,128)(2,1)} %all-gather.3.cloned.1.call-done), kind=kOutput, calls=%fused_computation | convolution fusion | flops 12884901888 | bytes 36700160 | tf_op jit(solution)/shard_map/dot_general | solution.py:32
  280.2 0.9 fusion.7
  281.2 0.9 fusion.15
  282.1 2.1 copy.11
  284.2 0.0 copy-start.2
  284.2 9.2 %fusion.2 = f32[32,16,512]{2,1,0:T(8,128)} fusion(bf16[512,32,16]{0,2,1:T(8,128)(2,1)} %bitcast.72, bf16[32,512,639]{2,1,0:T(8,128)(2,1)} %reshape.30), kind=kOutput, calls=%fused_computation.2 | convolution fusion | flops 268435456 | bytes 18350080 | tf_op jit(solution)/shard_map/fst,sfg->tfg/dot_general | solution.py:45
  293.4 2.6 copy.12
  296.0 0.0 copy-done.2
  296.0 2.5 fusion.14
  298.5 0.0 all-gather.5.cloned.1.call-update
  298.5 0.0 all-to-all-done
  298.6 78.9 %all-gather.5.cloned.1.call-done = bf16[512,8192]{1,0:T(8,128)(2,1)} async-done(((bf16[512,512]{1,0:T(8,128)(2,1)}), bf16[512,8192]{1,0:T(8,128)(2,1)}) %all-gather.5.cloned.1.call-update) | async-done | bytes 8388624 | tf_op jit(solution)/shard_map/all_gather | solution.py:56
  377.5 11.1 %fusion.9 = bf16[512,512]{1,0:T(8,128)(2,1)} fusion(bf16[512,8192]{1,0:T(8,128)(2,1)} %all-gather.5.cloned.1.call-done, bf16[8192,512]{1,0:T(8,128)(2,1)} %bitcast.30, bf16[512,512]{1,0:T(8,128)(2,1)} %param.7), kind=kOutput, calls=%fused_computation.14 | convolution fusion | flops 4295753728 | bytes 17825792 | tf_op jit(solution)/shard_map/dot_general | solution.py:55
  (3 shorter events, 0.0 us)
Async XLA Ops:
  6.5 254.1 %all-gather.3.cloned.1.call-start = ((), (), s32[]{:S(2)}) async-start(), calls=%async_computation.1 | async-start | bytes 8912896 | tf_op jit(solution)/shard_map/all_gather | solution.py:33
  74.9 223.6 %all-to-all-start = ((bf16[16,512,512]{2,1,0:T(8,128)(2,1)}), bf16[16,512,512]{2,1,0:T(8,128)(2,1)}, u32[]{:S(2)}, u32[]{:S(2)}) async-start(bf16[16,512,512]{2,1,0:T(8,128)(2,1)} %bitcast_dynamic-update-slice_fusion), calls=%async_computation | async-start | bytes 16777216 | tf_op jit(solution)/shard_map/all_to_all | solution.py:49
  79.8 33.6 %copy-start.1 = (bf16[32,128]{1,0:T(8,128)(2,1)S(1)}, bf16[32,128]{1,0:T(8,128)(2,1)}, u32[]{:S(2)}) copy-start(bf16[32,128]{1,0:T(8,128)(2,1)} %param.11) | copy-start | bytes 24580
  79.8 297.6 %all-gather.5.cloned.1.call-start = ((), (), s32[]{:S(2)}) async-start(), calls=%async_computation.2 | async-start | bytes 8912896 | tf_op jit(solution)/shard_map/all_gather | solution.py:56
  191.6 69.0 %copy-start = (f32[3,3,512]{2,1,0:T(4,128)S(1)}, f32[3,3,512]{2,1,0:T(4,128)}, u32[]{:S(2)}) copy-start(f32[3,3,512]{2,1,0:T(4,128)} %param.10) | copy-start | bytes 55300
  284.2 11.8 %copy-start.2 = (f32[512]{0:T(512)S(1)}, f32[512]{0:T(512)}, u32[]{:S(2)}) copy-start(f32[512]{0:T(512)} %param.12) | copy-start | bytes 6148
Sparse Core Ops, SparseCore 0:
  44.9 133.4 all-gather.2
  298.7 78.7 all-gather.4
